TPU v7x, 32 devices: a whole 2x2x4 slice. The times are simulated.
32 devices in a mesh: dp: 16 (over z, y, core), mp: 2 (over x).
Axes of the slice: x: 2, y: 2, z: 4, core: 2. Of those that a mesh axis runs over, the one named last changes fastest.
Arguments:
- hidden_in: bfloat16 [8192, 2048], P('dp', 'mp'), may hold values from -6 to 6
- doc_starts: int32 [16, 2], replicated, may hold values from 1 to 511, as said below
- attn_gain: bfloat16 [2048], P('dp'), may hold values from 0.25 to 1.75
- w_query: bfloat16 [2048, 2048], P('dp', 'mp'), may hold values from -0.125 to 0.125
- w_key: bfloat16 [2048, 512], P('dp', 'mp'), may hold values from -0.125 to 0.125
- w_value: bfloat16 [2048, 512], P('dp', 'mp'), may hold values from -0.125 to 0.125
- query_gain: bfloat16 [64], replicated, may hold values from 0.25 to 1.75
- key_gain: bfloat16 [64], replicated, may hold values from 0.25 to 1.75
- w_out: bfloat16 [2048, 2048], P('mp', 'dp'), may hold values from -0.5 to 0.5
- mlp_gain: bfloat16 [2048], P('dp'), may hold values from 0.25 to 1.75
- w_gate: bfloat16 [2048, 8192], P('dp', 'mp'), may hold values from -0.125 to 0.125
- w_up: bfloat16 [2048, 8192], P('dp', 'mp'), may hold values from -0.125 to 0.125
- w_down: bfloat16 [8192, 2048], P('mp', 'dp'), may hold values from -0.125 to 0.125
- cotangent: bfloat16 [8192, 2048], P('dp', 'mp'), may hold values from -12 to 12
Outputs:
- block_out: bfloat16 [8192, 2048], P('dp', 'mp')
- d_input: float32 [8192, 2048], P('dp', 'mp')
- d_attn_gain: float32 [2048], P('dp')
- d_query: float32 [2048, 2048], P('dp', 'mp')
- d_key: float32 [2048, 512], P('dp', 'mp')
- d_value: float32 [2048, 512], P('dp', 'mp')
- d_query_gain: float32 [64], replicated
- d_key_gain: float32 [64], replicated
- d_out_proj: float32 [2048, 2048], P('mp', 'dp')
- d_mlp_gain: float32 [2048], P('dp')
- d_gate: float32 [2048, 8192], P('dp', 'mp')
- d_up: float32 [2048, 8192], P('dp', 'mp')
- d_down: float32 [8192, 2048], P('mp', 'dp')
Inputs may be any that keep to these rules, and one draw needn't show every extreme that they name: `doc_starts`: in each row the first number is at most the second; documents may be empty.
All inputs are finite; a program needn't handle non-finite values.
Results may differ from a plain program's by a relative error of at most 0.017.
Values may be sent and summed in bfloat16 or wider, within the bound.
A program may use at most 256 MiB of HBM per device.

v0:
```python
from functools import partial
import math
import jax
import jax.numpy as jnp
from jax import lax
from jax.sharding import Mesh, PartitionSpec as P

BF = jnp.bfloat16
F32 = jnp.float32
EPS = 1e-05
TP = ("i", "m")
ALL = ("t", "i", "m")


def dot_f32(left, right, dims):
    return lax.dot_general(left, right, (dims, ((), ())), preferred_element_type=F32)


def nn(left, right):
    return dot_f32(left, right, ((1,), (0,)))


def nt(left, right):
    return dot_f32(left, right, ((1,), (1,)))


def tn(left, right):
    return dot_f32(left, right, ((0,), (0,)))


def rms_rows(v, gain):
    return v * lax.rsqrt(jnp.mean(v * v, axis=-1, keepdims=True) + EPS) * gain


def tables(cut_row, length, head_dim):
    position = jnp.arange(length, dtype=jnp.int32)
    doc = (position >= cut_row[0]).astype(jnp.int32) + (position >= cut_row[1]).astype(jnp.int32)
    starts = jnp.where(doc == 0, 0, jnp.where(doc == 1, cut_row[0], cut_row[1]))
    places = (position - starts).astype(F32)
    freqs = jnp.exp(-math.log(1000000.0) * 2.0 * jnp.arange(head_dim // 2, dtype=F32) / head_dim)
    angles = places[:, None] * freqs[None, :]
    angles = jnp.concatenate([angles, angles], axis=-1)
    allowed = (doc[:, None] == doc[None, :]) & (position[None, :] <= position[:, None])
    return (jnp.cos(angles), jnp.sin(angles), allowed)


def rotate(v, cosine, sine_table):
    halfway = v.shape[-1] // 2
    turned = jnp.concatenate([-v[..., halfway:], v[..., :halfway]], axis=-1)
    return v * cosine + turned * sine_table


def head_piece(pre, gain, cosine, sine_table):
    shaped = pre.reshape(pre.shape[0], -1, gain.shape[0])
    return rotate(rms_rows(shaped, gain), cosine, sine_table)


def attend(inputs, scale):
    queries, keys, values, allowed = inputs
    scores = jnp.einsum("qgd,td->gqt", queries, keys, preferred_element_type=F32) * scale
    scores = jnp.where(allowed[None], scores, -1e30)
    highest = jnp.max(scores, axis=-1, keepdims=True)
    weights_exp = jnp.exp(scores - highest)
    totals = jnp.sum(weights_exp, axis=-1, keepdims=True)
    probs = weights_exp / totals
    log_norm = highest[..., 0] + jnp.log(totals[..., 0])
    outputs = jnp.einsum("gqt,td->qgd", probs.astype(BF), values, preferred_element_type=F32)
    return (outputs.astype(BF), log_norm)


def attend_grad(inputs, scale):
    queries, keys, values, d_outputs, log_norm, allowed = inputs
    scores = jnp.einsum("qgd,td->gqt", queries, keys, preferred_element_type=F32) * scale
    scores = jnp.where(allowed[None], scores, -1e30)
    probs = jnp.exp(scores - log_norm[..., None])
    d_probs = jnp.einsum("qgd,td->gqt", d_outputs, values, preferred_element_type=F32)
    inner_sum = jnp.sum(probs * d_probs, axis=-1, keepdims=True)
    d_scores = (probs * (d_probs - inner_sum)).astype(BF)
    d_queries = jnp.einsum("gqt,td->qgd", d_scores, keys, preferred_element_type=F32) * scale
    d_keys = jnp.einsum("gqt,qgd->td", d_scores, queries, preferred_element_type=F32) * scale
    d_values = jnp.einsum("gqt,qgd->td", probs.astype(BF), d_outputs, preferred_element_type=F32)
    return (d_queries, d_keys, d_values)


def gather_pieces(piece, ranks):
    rows, cols = piece.shape
    parts = lax.all_gather(piece, TP, axis=0)
    parts = parts.reshape(ranks[0], ranks[1], rows, cols)
    return jnp.moveaxis(parts, 1, 2).reshape(ranks[0] * rows, ranks[1] * cols)


def scatter_pieces(partial_sum, ranks):
    rows, cols = partial_sum.shape
    parts = partial_sum.astype(BF).reshape(ranks[0], rows // ranks[0], ranks[1], cols // ranks[1])
    parts = jnp.moveaxis(parts, 2, 1).reshape(-1, rows // ranks[0], cols // ranks[1])
    mine = lax.psum_scatter(parts, TP, scatter_dimension=0, tiled=False)
    return mine.astype(F32)


def spread(local, inner):
    rows, cols = local.shape
    parts = jnp.moveaxis(local.reshape(rows, inner, cols // inner), 1, 0)
    parts = lax.all_to_all(parts, "i", 0, 0, tiled=False)
    return parts.reshape(inner * rows, cols // inner)


def collect(block, inner):
    rows, cols = block.shape
    parts = lax.all_to_all(block.reshape(inner, rows // inner, cols), "i", 0, 0, tiled=False)
    return jnp.moveaxis(parts, 0, 1).reshape(rows // inner, inner * cols)


def full_rows(local, inner):
    return lax.all_gather(spread(local, inner), "t", axis=0, tiled=True)


def grad_rows(part, inner):
    mine = lax.psum_scatter(part.astype(BF), "t", scatter_dimension=0, tiled=True)
    return collect(mine, inner).astype(F32)


def body(
    hidden_in,
    doc_starts,
    attn_gain,
    w_query,
    w_key,
    w_value,
    query_gain,
    key_gain,
    w_out,
    mlp_gain,
    w_gate,
    w_up,
    w_down,
    cotangent,
    *,
    groups,
    inner,
    halves
):
    length, width_part = hidden_in.shape
    ranks = (inner, halves)
    width = width_part * halves
    head_dim = query_gain.shape[0]
    scale = head_dim ** (-0.5)
    t_index, m_index = (lax.axis_index("t"), lax.axis_index("m"))
    cuts = lax.dynamic_slice_in_dim(doc_starts, t_index * inner, inner, 0)
    cosine, sine_table, allowed = jax.vmap(partial(tables, length=length, head_dim=head_dim))(cuts)
    cosine = cosine.reshape(inner * length, 1, head_dim)
    sine_table = sine_table.reshape(inner * length, 1, head_dim)
    q_gain, k_gain = (query_gain.astype(F32), key_gain.astype(F32))
    gains = lax.all_gather(jnp.stack([attn_gain, mlp_gain], 1), ("t", "i"), axis=0, tiled=True)
    gain_one, gain_two = (gains[:, 0].astype(F32), gains[:, 1].astype(F32))
    full_in = gather_pieces(hidden_in, ranks)
    sizes = [w.shape[1] // inner for w in (w_query, w_key, w_value)] + [w_out.shape[0] // inner]
    edges = [sum(sizes[:n]) for n in range(5)]

    def by_rank(w):
        return w.reshape(w.shape[0], inner, w.shape[1] // inner)

    attn_local = jnp.concatenate(
        [by_rank(w_query), by_rank(w_key), by_rank(w_value), by_rank(w_out.T)], 2
    )
    attn_cols = full_rows(attn_local.reshape(attn_local.shape[0], -1), inner)
    query_cols, key_cols, value_cols, out_t = [
        attn_cols[:, edges[n] : edges[n + 1]] for n in range(4)
    ]
    resid = full_in.astype(F32)
    r_one = lax.rsqrt(jnp.mean(resid * resid, axis=-1, keepdims=True) + EPS)
    normed_one = (resid * r_one * gain_one).astype(BF)
    gate_cols = full_rows(w_gate, inner)
    up_cols = full_rows(w_up, inner)
    down_t = full_rows(w_down.T, inner)
    grad_full = gather_pieces(cotangent, ranks)
    query_pre = nn(normed_one, query_cols)
    key_pre = nn(normed_one, key_cols)
    value_low = nn(normed_one, value_cols).astype(BF)
    query_rot = head_piece(query_pre, q_gain, cosine, sine_table).astype(BF)
    key_rot = head_piece(key_pre, k_gain, cosine, sine_table).astype(BF)
    group = query_rot.shape[1]
    query_stack = query_rot.reshape(inner, length, group, head_dim)
    key_stack = key_rot.reshape(inner, length, head_dim)
    value_stack = value_low.reshape(inner, length, head_dim)
    attended, log_norm = lax.map(
        partial(attend, scale=scale), (query_stack, key_stack, value_stack, allowed)
    )
    mixed = attended.reshape(inner * length, group * head_dim)
    middle = hidden_in.astype(F32) + scatter_pieces(nt(mixed, out_t), ranks)
    my_gain_one = lax.dynamic_slice_in_dim(gain_one, m_index * width_part, width_part, 0)
    my_gain_two = lax.dynamic_slice_in_dim(gain_two, m_index * width_part, width_part, 0)
    r_two = lax.rsqrt(lax.psum(jnp.sum(middle * middle, axis=-1, keepdims=True), "m") / width + EPS)
    normed_two = gather_pieces((middle * r_two * my_gain_two).astype(BF), ranks)
    gate_pre, up_pre = (nn(normed_two, gate_cols), nn(normed_two, up_cols))
    d_inner = nn(grad_full, down_t)
    sigmoid_gate = jax.nn.sigmoid(gate_pre)
    inner_act = (gate_pre * sigmoid_gate * up_pre).astype(BF)
    d_gate_pre = (d_inner * up_pre * sigmoid_gate * (1.0 + gate_pre * (1.0 - sigmoid_gate))).astype(
        BF
    )
    d_up_pre = (d_inner * gate_pre * sigmoid_gate).astype(BF)
    d_normed_two = scatter_pieces(nt(d_gate_pre, gate_cols) + nt(d_up_pre, up_cols), ranks)
    mlp_out = scatter_pieces(nt(inner_act, down_t), ranks)
    block_out = (middle + mlp_out).astype(BF)
    scaled = d_normed_two * my_gain_two
    dot_two = lax.psum(jnp.sum(scaled * middle, axis=-1, keepdims=True), "m") / width
    d_gain_two = jnp.sum(d_normed_two * middle * r_two, axis=0)
    d_middle = cotangent.astype(F32) + r_two * scaled - middle * (r_two * r_two * r_two) * dot_two
    d_middle_low = gather_pieces(d_middle.astype(BF), ranks)
    d_gate = grad_rows(tn(normed_two, d_gate_pre), inner)
    d_up = grad_rows(tn(normed_two, d_up_pre), inner)
    d_down = grad_rows(tn(grad_full, inner_act), inner).T
    d_mixed = nn(d_middle_low, out_t).astype(BF)
    d_out_part = tn(d_middle_low, mixed)
    d_mixed_stack = d_mixed.reshape(inner, length, group, head_dim)
    d_query_stack, d_key_stack, d_value_stack = lax.map(
        partial(attend_grad, scale=scale),
        (query_stack, key_stack, value_stack, d_mixed_stack, log_norm, allowed),
    )
    rotary_piece = partial(head_piece, cosine=cosine, sine_table=sine_table)
    _, query_pull = jax.vjp(rotary_piece, query_pre, q_gain)
    d_query_pre, d_qgain_part = query_pull(d_query_stack.reshape(inner * length, group, head_dim))
    _, key_pull = jax.vjp(rotary_piece, key_pre, k_gain)
    d_key_pre, d_kgain_part = key_pull(d_key_stack.reshape(inner * length, 1, head_dim))
    d_heads = jnp.concatenate(
        [d_query_pre, d_key_pre, d_value_stack.reshape(inner * length, head_dim)], 1
    ).astype(BF)
    heads_cols = attn_cols[:, : edges[3]]
    d_normed_one = scatter_pieces(nt(d_heads, heads_cols), ranks)
    d_attn = jnp.concatenate([tn(normed_one, d_heads), d_out_part], 1)
    d_attn = grad_rows(d_attn, inner).reshape(-1, inner, edges[4])
    d_query, d_key, d_value, d_out_t = [
        d_attn[:, :, edges[n] : edges[n + 1]].reshape(d_attn.shape[0], -1) for n in range(4)
    ]
    mine = hidden_in.astype(F32)
    i_index = lax.axis_index("i")
    r_own = lax.dynamic_slice_in_dim(r_one, i_index * length, length, 0)
    scaled = d_normed_one * my_gain_one
    dot_one = lax.psum(jnp.sum(scaled * mine, axis=-1, keepdims=True), "m") / width
    d_gain_one = jnp.sum(d_normed_one * mine * r_own, axis=0)
    d_input = d_middle + r_own * scaled - mine * (r_own * r_own * r_own) * dot_one
    both = jnp.stack([d_gain_one, d_gain_two], 0)
    wide = lax.dynamic_update_slice(jnp.zeros((2, width), F32), both, (0, m_index * width_part))
    small = jnp.concatenate([wide.reshape(-1), d_qgain_part, d_kgain_part])
    small = lax.psum(small, ALL)
    wide = small[: 2 * width].reshape(2, width)
    shard = attn_gain.shape[0]
    own = lax.dynamic_slice(wide, (0, (t_index * inner + i_index) * shard), (2, shard))
    return (
        block_out,
        d_input,
        own[0],
        d_query,
        d_key,
        d_value,
        small[2 * width : 2 * width + head_dim],
        small[2 * width + head_dim :],
        d_out_t.T,
        own[1],
        d_gate,
        d_up,
        d_down,
    )


def solution(mesh):
    dp, halves = (mesh.shape["dp"], mesh.shape["mp"])
    inner = 4
    groups = dp // inner
    fine = Mesh(mesh.devices.reshape(groups, inner, halves), ("t", "i", "m"))
    rows = P(("t", "i"))
    block = P(("t", "i"), "m")
    turned = P("m", ("t", "i"))
    return jax.shard_map(
        partial(body, groups=groups, inner=inner, halves=halves),
        mesh=fine,
        in_specs=(
            block,
            P(),
            rows,
            block,
            block,
            block,
            P(),
            P(),
            turned,
            rows,
            block,
            block,
            turned,
            block,
        ),
        out_specs=(
            block,
            block,
            rows,
            block,
            block,
            block,
            P(),
            P(),
            turned,
            rows,
            block,
            block,
            turned,
        ),
        check_vma=False,
    )
```

profile of v0, /device:TPU:0, one launch (start us, length us, event | category | flops | bytes accessed | tf_op | source)
XLA Modules:
  0.0 1419.3 jit_solution(7471907104294036596)
XLA Ops:
  27.7 20.5 %all_gather.41 = bf16[2048,2]{0,1:T(2,128)(2,1)S(1)} all-gather(bf16[128,2]{0,1:T(2,128)(2,1)S(1)} %pad_maximum_fusion.6), channel_id=1, replica_groups=mesh['t'=4,'i'=4,'m'=2] {'t','i'}, dimensions={0}, use_global_device_ids=true | all-gather | bytes 8704 | tf_op jit(solution)/shard_map/all_gather | solution.py:153
  50.1 31.7 %all-gather.13.cloned.1.call-done = bf16[2048,640]{0,1:T(8,128)(2,1)} async-done(((bf16[512,640]{0,1:T(8,128)(2,1)}), bf16[2048,640]{0,1:T(8,128)(2,1)}) %all-gather.13.cloned.1.call-update) | async-done | bytes 2621456 | tf_op jit(solution)/shard_map/all_gather | solution.py:114
  81.8 55.0 %all-gather.21.cloned.1.call-done = bf16[4096,1024]{1,0:T(8,128)(2,1)} async-done(((bf16[512,1024]{1,0:T(8,128)(2,1)}), bf16[4096,1024]{1,0:T(8,128)(2,1)}) %all-gather.21.cloned.1.call-update) | async-done | bytes 8388624 | tf_op jit(solution)/shard_map/all_gather | solution.py:87
  153.9 27.7 %copy.137 = f32[4,2,512,1024]{3,1,2,0:T(2,128)S(1)} copy(f32[4,2,512,1024]{3,2,1,0:T(8,128)} %bitcast_convert_fusion) | data formatting | bytes 33554432 | tf_op jit(solution)/shard_map/convert_element_type | solution.py:169
  203.6 16.4 %copy.142 = bf16[4,512,2,1024]{3,2,1,0:T(2,128)(2,1)} copy(bf16[4,512,2,1024]{3,1,2,0:T(8,128)(2,1)} %fusion.58) | data formatting | bytes 16777216 | tf_op jit(solution)/shard_map/mul | solution.py:171
  220.1 14.8 %reshape.761 = bf16[2048,2048,1]{1,0,2:T(8,128)(2,1)} reshape(bf16[4,512,2,1024]{3,2,1,0:T(2,128)(2,1)} %copy.142) | data formatting | bytes 16777216 | tf_op jit(solution)/shard_map/convert_element_type | solution.py:171
  250.3 18.6 %while.26 = (s32[]{:T(128)}, bf16[4,512,4,64]{1,3,2,0:T(8,128)(2,1)}, f32[4,4,512]{2,1,0:T(4,128)}, bf16[4,512,64]{1,2,0:T(8,128)(2,1)S(1)}, pred[4,512,512]{1,2...) while((s32[]{:T(128)}, ...), condition=%wide.region_6.7_spmd, body=%wide.region_3.6_spmd.sunk | while | flops 281147392 | bytes 14617177 | solution.py:185
  278.9 14.5 %reshape.696 = bf16[4,512,2,1024]{3,2,1,0:T(2,128)(2,1)} reshape(bf16[2048,2048]{1,0:T(8,128)(2,1)} %convolution_convert_fusion.2) | data formatting | bytes 16777216 | tf_op jit(solution)/shard_map/reshape | solution.py:94
  303.4 70.8 %reduce-scatter.9.cloned.1.call-done = bf16[1,512,1024]{2,1,0:T(8,128)(2,1)} async-done(((bf16[8,512,1024]{2,1,0:T(8,128)(2,1)}), bf16[1,512,1024]{2,1,0:T(8,128)(2,1)}) %reduce-scatter.9.cloned.1.call-update) | async-done | bytes 1048592 | tf_op jit(solution)/shard_map/reduce_scatter | solution.py:96
  384.2 25.4 %all_to_all.41 = bf16[4,128,1024]{1,2,0:T(8,128)(2,1)S(1)} all-to-all(bf16[4,128,1024]{1,2,0:T(8,128)(2,1)S(1)} %bitcast.453), channel_id=1, replica_groups=mesh['t'=4,'i'=4,'m'=2] {'i'}, dimensions={0} | all-to-all | bytes 2097152 | tf_op jit(solution)/shard_map/all_to_all | solution.py:103
  412.6 28.4 %all_to_all.42 = bf16[4,128,1024]{1,2,0:T(8,128)(2,1)S(1)} all-to-all(bf16[4,128,1024]{1,2,0:T(8,128)(2,1)S(1)} %bitcast.454), channel_id=1, replica_groups=mesh['t'=4,'i'=4,'m'=2] {'i'}, dimensions={0} | all-to-all | bytes 2097152 | tf_op jit(solution)/shard_map/all_to_all | solution.py:103
  442.4 18.0 %all_to_all.43 = bf16[4,128,1024]{1,2,0:T(8,128)(2,1)S(1)} all-to-all(bf16[4,128,1024]{1,2,0:T(8,128)(2,1)} %bitcast.462), channel_id=1, replica_groups=mesh['t'=4,'i'=4,'m'=2] {'i'}, dimensions={0} | all-to-all | bytes 2097152 | tf_op jit(solution)/shard_map/all_to_all | solution.py:103
  461.8 16.7 %copy.155 = bf16[4,2,512,1024]{3,1,2,0:T(2,128)(2,1)} copy(bf16[4,2,512,1024]{3,2,1,0:T(8,128)(2,1)} %bitcast.439) | data formatting | bytes 16777216 | tf_op jit(solution)/shard_map/reshape | solution.py:88
  489.4 18.2 %all-gather.23.cloned.1.call-done = bf16[4096,1024]{1,0:T(8,128)(2,1)} async-done(((bf16[512,1024]{1,0:T(8,128)(2,1)}), bf16[4096,1024]{1,0:T(8,128)(2,1)}) %all-gather.23.cloned.1.call-update) | async-done | bytes 8388624 | tf_op jit(solution)/shard_map/all_gather | solution.py:87
  507.5 16.4 %copy.148 = bf16[4,2,512,1024]{3,1,2,0:T(2,128)(2,1)} copy(bf16[4,2,512,1024]{3,2,1,0:T(8,128)(2,1)} %bitcast.444) | data formatting | bytes 16777216 | tf_op jit(solution)/shard_map/reshape | solution.py:88
  534.2 56.2 %all-gather.15.cloned.1.call-done = bf16[2048,1024]{1,0:T(8,128)(2,1)} async-done(((bf16[512,1024]{1,0:T(8,128)(2,1)}), bf16[2048,1024]{1,0:T(8,128)(2,1)}) %all-gather.15.cloned.1.call-update) | async-done | bytes 4194320 | tf_op jit(solution)/shard_map/all_gather | solution.py:114
  590.4 14.7 %fusion.116 = f32[2048,1024]{1,0:T(8,128)} fusion(bf16[2048,2048]{1,0:T(8,128)(2,1)} %bitcast.440, bf16[2048,1024]{1,0:T(8,128)(2,1)} %all-gather.15.cloned.1.call-done), kind=kOutput, calls=%fused_computation.219 | convolution fusion | flops 8589934592 | bytes 20971520 | tf_op jit(solution)/shard_map/dot_general | solution.py:16
  605.1 66.3 %all-gather.17.cloned.1.call-done = bf16[2048,1024]{1,0:T(8,128)(2,1)} async-done(((bf16[512,1024]{1,0:T(8,128)(2,1)}), bf16[2048,1024]{1,0:T(8,128)(2,1)}) %all-gather.17.cloned.1.call-update) | async-done | bytes 4194320 | tf_op jit(solution)/shard_map/all_gather | solution.py:114
  671.4 14.4 %fusion.117 = f32[2048,1024]{1,0:T(8,128)} fusion(bf16[2048,2048]{1,0:T(8,128)(2,1)} %bitcast.441, bf16[2048,1024]{1,0:T(8,128)(2,1)} %all-gather.17.cloned.1.call-done), kind=kOutput, calls=%fused_computation.220 | convolution fusion | flops 8589934592 | bytes 20971520 | tf_op jit(solution)/shard_map/dot_general | solution.py:16
  685.8 66.6 %all-gather.19.cloned.1.call-done = bf16[2048,1024]{1,0:T(8,128)(2,1)} async-done(((bf16[512,1024]{1,0:T(8,128)(2,1)}), bf16[2048,1024]{1,0:T(8,128)(2,1)}) %all-gather.19.cloned.1.call-update) | async-done | bytes 4194320 | tf_op jit(solution)/shard_map/all_gather | solution.py:114
  752.4 21.8 %multiply_convert_fusion.2 = (bf16[2048,1024]{1,0:T(8,128)(2,1)}, bf16[2048,1024]{1,0:T(8,128)(2,1)}, bf16[2048,1024]{1,0:T(8,128)(2,1)}) fusion(f32[2048,1024]{1,0:T(8,128)} %fusion.116, f32[2048,1024]{1,0:T(8,128)} %fusion.117, bf16[2048,2048]{1,0:T(8,128)(2,1)} %bitcast.437, bf16[2048,1024]{1,0:T(8,128)(2,1)} %all-gather.19.cloned.1.call-done), kind=kOutput, calls=%fused_computation.70 | convolution fusion | flops 8623489024 | bytes 41943040 | tf_op jit(solution)/shard_map/dot_general | solution.py:16
  788.6 16.4 %add_convert_fusion = bf16[2048,2048]{1,0:T(8,128)(2,1)} fusion(f32[2048,2048]{1,0:T(8,128)} %fusion.118, bf16[2048,1024]{1,0:T(8,128)(2,1)} %get-tuple-element.269, bf16[2048,1024]{1,0:T(8,128)(2,1)} %all-gather.17.cloned.1.call-done), kind=kOutput, calls=%fused_computation.65 | convolution fusion | flops 8598323200 | bytes 33554432 | tf_op jit(solution)/shard_map/dot_general | solution.py:16
  805.0 14.5 %reshape.710 = bf16[4,512,2,1024]{3,2,1,0:T(2,128)(2,1)} reshape(bf16[2048,2048]{1,0:T(8,128)(2,1)} %add_convert_fusion) | data formatting | bytes 16777216 | tf_op jit(solution)/shard_map/reshape | solution.py:94
  828.9 69.9 %reduce-scatter.13.cloned.1.call-done = bf16[1,512,1024]{2,1,0:T(8,128)(2,1)} async-done(((bf16[8,512,1024]{2,1,0:T(8,128)(2,1)}), bf16[1,512,1024]{2,1,0:T(8,128)(2,1)}) %reduce-scatter.13.cloned.1.call-update) | async-done | bytes 1048592 | tf_op jit(solution)/shard_map/reduce_scatter | solution.py:96
  938.8 14.5 %convert_bitcast_fusion = bf16[2048,1024]{0,1:T(8,128)(2,1)} fusion(bf16[2048,1024]{1,0:T(8,128)(2,1)} %get-tuple-element.271, bf16[2048,2048]{1,0:T(8,128)(2,1)} %bitcast.438), kind=kOutput, calls=%fused_computation.77 | convolution fusion | flops 8592031744 | bytes 16777216 | tf_op jit(solution)/shard_map/dot_general | solution.py:16
  964.9 16.4 %copy.157 = bf16[4,2,512,1024]{3,1,2,0:T(2,128)(2,1)} copy(bf16[4,2,512,1024]{3,2,1,0:T(8,128)(2,1)} %bitcast.445) | data formatting | bytes 16777216 | tf_op jit(solution)/shard_map/reshape | solution.py:88
  1004.3 116.4 %while.27 = (s32[]{:T(128)}, f32[4,512,4,64]{1,0,3,2:T(4,128)}, f32[4,512,64]{1,0,2:T(4,128)}, bf16[4,512,64]{1,2,0:T(8,128)(2,1)}, bf16[4,512,64]{1,2,0:T(8,128...) while((s32[]{:T(128)}, f32[4,512,4,64]{1,0,3,2:T(4,128)}, ...), condition=%wide.region_16.17_spmd, body=%wide.region_14.16_spmd.sunk | while | flops 686979072 | bytes 54259364 | solution.py:216
  1154.6 14.5 %reshape.721 = bf16[4,512,2,1024]{3,2,1,0:T(2,128)(2,1)} reshape(bf16[2048,2048]{1,0:T(8,128)(2,1)} %convolution_convert_fusion) | data formatting | bytes 16777216 | tf_op jit(solution)/shard_map/reshape | solution.py:94
  1192.8 14.5 %reshape.706 = bf16[4,512,2,1024]{3,2,1,0:T(2,128)(2,1)} reshape(bf16[2048,2048]{1,0:T(8,128)(2,1)} %convolution_convert_fusion.1) | data formatting | bytes 16777216 | tf_op jit(solution)/shard_map/reshape | solution.py:94
  1293.1 39.7 %reduce-scatter.15.cloned.1.call-done = bf16[1,512,1024]{2,1,0:T(8,128)(2,1)} async-done(((bf16[8,512,1024]{2,1,0:T(8,128)(2,1)}), bf16[1,512,1024]{2,1,0:T(8,128)(2,1)}) %reduce-scatter.15.cloned.1.call-update) | async-done | bytes 1048592 | tf_op jit(solution)/shard_map/reduce_scatter | solution.py:96
  1335.0 39.7 %psum.31 = f32[4224]{0:T(1024)S(1)} all-reduce(f32[4224]{0:T(1024)S(1)} %concatenate.65), channel_id=1, replica_groups=mesh['t'=4,'i'=4,'m'=2] {'t','i','m'}, use_global_device_ids=true, to_apply=%region_26.27 | all-reduce | flops 4224 | bytes 33792 | tf_op jit(solution)/shard_map/psum | solution.py:245
  1381.1 26.9 %reduce-scatter.11.cloned.1.call-done = bf16[1,512,1024]{2,1,0:T(8,128)(2,1)} async-done(((bf16[8,512,1024]{2,1,0:T(8,128)(2,1)}), bf16[1,512,1024]{2,1,0:T(8,128)(2,1)}) %reduce-scatter.11.cloned.1.call-update) | async-done | bytes 1048592 | tf_op jit(solution)/shard_map/reduce_scatter | solution.py:96
  (397 shorter events, 521.2 us)
Async XLA Ops:
  7.2 74.5 %all-gather.13.cloned.1.call-start = ((), (), s32[]{:S(2)}) async-start(), calls=%async_computation.16 | async-start | bytes 3276800 | tf_op jit(solution)/shard_map/all_gather | solution.py:114
  26.6 110.3 %all-gather.21.cloned.1.call-start = ((), (), s32[]{:S(2)}) async-start(), calls=%async_computation.28 | async-start | bytes 9437184 | tf_op jit(solution)/shard_map/all_gather | solution.py:87
  27.3 346.9 %reduce-scatter.9.cloned.1.call-start = ((), (), s32[]{:S(2)}) async-start(), calls=%async_computation.17 | async-start | bytes 9437184 | tf_op jit(solution)/shard_map/reduce_scatter | solution.py:96
  27.6 213.8 %copy-start.60 = (f32[64]{0:T(128)}, f32[64]{0:T(128)S(1)}, u32[]{:S(2)}) copy-start(f32[64]{0:T(128)S(1)} %convert_element_type.239) | copy-start | bytes 772
  48.2 196.1 %copy-start.58 = (f32[64]{0:T(128)}, f32[64]{0:T(128)S(1)}, u32[]{:S(2)}) copy-start(f32[64]{0:T(128)S(1)} %convert_element_type.247) | copy-start | bytes 772
  49.2 138.4 %copy-start.48 = (f32[2048,1]{0,1:T(1,128)}, f32[2048,1]{0,1:T(1,128)S(1)}, u32[]{:S(2)}) copy-start(f32[2048,1]{0,1:T(1,128)S(1)} %get-tuple-element.297) | copy-start | bytes 24580
  302.7 159.0 %all-gather.25.cloned.1.call-start = ((), (), s32[]{:S(2)}) async-start(), calls=%async_computation.30 | async-start | bytes 9437184 | tf_op jit(solution)/shard_map/all_gather | solution.py:87
  303.3 204.2 %all-gather.23.cloned.1.call-start = ((), (), s32[]{:S(2)}) async-start(), calls=%async_computation.29 | async-start | bytes 9437184 | tf_op jit(solution)/shard_map/all_gather | solution.py:87
  303.4 603.3 %copy-start.44 = (f32[1024,1]{0,1:T(1,128)}, f32[1024,1]{0,1:T(1,128)S(1)}, u32[]{:S(2)}) copy-start(f32[1024,1]{0,1:T(1,128)S(1)} %dynamic-slice_convert_fusion) | copy-start | bytes 12292
  380.8 525.9 %copy-start.50 = (f32[512,1]{0,1:T(1,128)}, f32[512,1]{0,1:T(1,128)S(1)}, u32[]{:S(2)}) copy-start(f32[512,1]{0,1:T(1,128)S(1)} %get-tuple-element.264) | copy-start | bytes 6148
  380.8 525.9 %copy-start.53 = (f32[512,1]{0,1:T(1,128)}, f32[512,1]{0,1:T(1,128)S(1)}, u32[]{:S(2)}) copy-start(f32[512,1]{0,1:T(1,128)S(1)} %get-tuple-element.263) | copy-start | bytes 6148
  383.4 207.0 %all-gather.15.cloned.1.call-start = ((), (), s32[]{:S(2)}) async-start(), calls=%async_computation.18 | async-start | bytes 5242880 | tf_op jit(solution)/shard_map/all_gather | solution.py:114
  410.9 260.5 %all-gather.17.cloned.1.call-start = ((), (), s32[]{:S(2)}) async-start(), calls=%async_computation.19 | async-start | bytes 5242880 | tf_op jit(solution)/shard_map/all_gather | solution.py:114
  442.3 310.0 %all-gather.19.cloned.1.call-start = ((), (), s32[]{:S(2)}) async-start(), calls=%async_computation.20 | async-start | bytes 5242880 | tf_op jit(solution)/shard_map/all_gather | solution.py:114
  461.7 437.2 %reduce-scatter.13.cloned.1.call-start = ((), (), s32[]{:S(2)}) async-start(), calls=%async_computation.22 | async-start | bytes 9437184 | tf_op jit(solution)/shard_map/reduce_scatter | solution.py:96
  828.9 136.0 %all-gather.27.cloned.1.call-start = ((), (), s32[]{:S(2)}) async-start(), calls=%async_computation.31 | async-start | bytes 9437184 | tf_op jit(solution)/shard_map/all_gather | solution.py:87
  910.3 306.3 %reduce-scatter.21.cloned.1.call-start = ((), (), s32[]{:S(2)}) async-start(), calls=%async_computation.26 | async-start | bytes 5242880 | tf_op jit(solution)/shard_map/reduce_scatter | solution.py:118
  924.5 295.9 %reduce-scatter.19.cloned.1.call-start = ((), (), s32[]{:S(2)}) async-start(), calls=%async_computation.25 | async-start | bytes 5242880 | tf_op jit(solution)/shard_map/reduce_scatter | solution.py:118
  938.5 299.8 %reduce-scatter.23.cloned.1.call-start = ((), (), s32[]{:S(2)}) async-start(), calls=%async_computation.27 | async-start | bytes 5242880 | tf_op jit(solution)/shard_map/reduce_scatter | solution.py:118
  953.3 304.8 %reduce-scatter.17.cloned.1.call-start = ((), (), s32[]{:S(2)}) async-start(), calls=%async_computation.24 | async-start | bytes 3276800 | tf_op jit(solution)/shard_map/reduce_scatter | solution.py:118
  1145.6 187.2 %reduce-scatter.15.cloned.1.call-start = ((), (), s32[]{:S(2)}) async-start(), calls=%async_computation.23 | async-start | bytes 9437184 | tf_op jit(solution)/shard_map/reduce_scatter | solution.py:96
  1178.5 229.5 %reduce-scatter.11.cloned.1.call-start = ((), (), s32[]{:S(2)}) async-start(), calls=%async_computation.21 | async-start | bytes 9437184 | tf_op jit(solution)/shard_map/reduce_scatter | solution.py:96
  1216.7 18.1 %all-to-all-start.6 = ((bf16[4,128,1024]{2,1,0:T(8,128)(2,1)}), bf16[4,128,1024]{2,1,0:T(8,128)(2,1)S(1)}, u32[]{:S(2)}, u32[]{:S(2)}) async-start(bf16[4,128,1024]{2,1,0:T(8,128)(2,1)} %bitcast.464), calls=%async_computation.13 | async-start | bytes 2097152 | tf_op jit(solution)/shard_map/all_to_all | solution.py:109
  1234.8 18.0 %all-to-all-start.5 = ((bf16[4,128,1024]{2,1,0:T(8,128)(2,1)}), bf16[4,128,1024]{2,1,0:T(8,128)(2,1)S(1)}, u32[]{:S(2)}, u32[]{:S(2)}) async-start(bf16[4,128,1024]{2,1,0:T(8,128)(2,1)} %bitcast.463), calls=%async_computation.11 | async-start | bytes 2097152 | tf_op jit(solution)/shard_map/all_to_all | solution.py:109
  1252.7 18.0 %all-to-all-start.7 = ((bf16[4,128,1024]{1,2,0:T(8,128)(2,1)}), bf16[4,128,1024]{1,2,0:T(8,128)(2,1)S(1)}, u32[]{:S(2)}, u32[]{:S(2)}) async-start(bf16[4,128,1024]{1,2,0:T(8,128)(2,1)} %copy_bitcast_fusion), calls=%async_computation.15 | async-start | bytes 2097152 | tf_op jit(solution)/shard_map/all_to_all | solution.py:109
  1270.7 14.5 %all-to-all-start.4 = ((bf16[4,128,640]{1,2,0:T(8,128)(2,1)}), bf16[4,128,640]{1,2,0:T(8,128)(2,1)}, u32[]{:S(2)}, u32[]{:S(2)}) async-start(bf16[4,128,640]{1,2,0:T(8,128)(2,1)} %copy_bitcast_fusion.3), calls=%async_computation.9 | async-start | bytes 1310720 | tf_op jit(solution)/shard_map/all_to_all | solution.py:109
  1279.8 128.2 %copy-start.9 = (bf16[1,512,1024]{2,1,0:T(8,128)(2,1)S(1)}, bf16[1,512,1024]{2,1,0:T(8,128)(2,1)}, u32[]{:S(2)}) copy-start(bf16[1,512,1024]{2,1,0:T(8,128)(2,1)} %reduce-scatter.9.cloned.1.call-done) | copy-start | bytes 3145732
  1279.8 128.2 %copy-start.15 = (bf16[512,1024]{1,0:T(8,128)(2,1)S(1)}, bf16[512,1024]{1,0:T(8,128)(2,1)}, u32[]{:S(2)}) copy-start(bf16[512,1024]{1,0:T(8,128)(2,1)} %param.31) | copy-start | bytes 3145732
  1279.8 128.2 %copy-start.45 = (f32[1024,1]{0,1:T(1,128)S(1)}, f32[1024,1]{0,1:T(1,128)}, u32[]{:S(2)}) copy-start(f32[1024,1]{0,1:T(1,128)} %copy-done.44) | copy-start | bytes 12292
  1279.8 128.2 %copy-start.51 = (f32[512,1]{0,1:T(1,128)S(1)}, f32[512,1]{0,1:T(1,128)}, u32[]{:S(2)}) copy-start(f32[512,1]{0,1:T(1,128)} %copy-done.50) | copy-start | bytes 6148
  1279.8 128.2 %copy-start.54 = (f32[512,1]{0,1:T(1,128)S(1)}, f32[512,1]{0,1:T(1,128)}, u32[]{:S(2)}) copy-start(f32[512,1]{0,1:T(1,128)} %copy-done.53) | copy-start | bytes 6148
  1279.8 128.2 %copy-start.56 = (f32[512,1]{0,1:T(1,128)S(1)}, f32[512,1]{0,1:T(1,128)}, u32[]{:S(2)}) copy-start(f32[512,1]{0,1:T(1,128)} %copy-done.55) | copy-start | bytes 6148
  (65 other events, 951.9 us)
Sparse Core Ops, SparseCore 0:
  26.7 55.0 all-gather.12
  83.7 53.1 all-gather.20
  302.9 71.2 reduce-scatter.8
  376.1 74.5 all-gather.24
  453.1 54.3 all-gather.22
  509.6 80.7 all-gather.14
  592.1 79.2 all-gather.16
  673.0 79.2 all-gather.18
  829.0 69.8 reduce-scatter.12
  910.4 54.3 all-gather.26
  967.2 76.7 reduce-scatter.20
  1046.2 77.2 reduce-scatter.18
  1125.8 77.2 reduce-scatter.22
  1205.4 52.5 reduce-scatter.16
  1261.7 70.9 reduce-scatter.14
  1336.1 71.9 reduce-scatter.10
where the time goes:
time: 1430 us; the launch traced here: 1420 us
  waiting for transfers between devices  558 us (39%)
  local copies, waits for them, and re-layouts  361 us (25%)
  matrix products  229 us (16%)
  blocking collectives  162 us (11%)
  other arithmetic  76.3 us (5%)
  starting transfers between devices  15.8 us (1%)
  between operations  15.6 us (1%)
    all_gather x4, waiting for transfers between devices, full_rows(): return lax.all_gather(spread(local, inner), 't', axis=0, tiled=True)  221 us
    reduce_scatter x4, waiting for transfers between devices, scatter_pieces(): mine = lax.psum_scatter(parts, TP, scatter_dimension=0, tiled=False)  207 us
    dot_general x17, matrix products, dot_f32(): lax.dot_general(left, right, (dims, ((), ())), preferred_element_type=F32)  176 us
    all_to_all x4, blocking collectives, spread(): parts = lax.all_to_all(parts, 'i', 0, 0, tiled=False)  86.1 us
    all_gather x4, waiting for transfers between devices, gather_pieces(): parts = lax.all_gather(piece, TP, axis=0)  84.7 us
    dynamic_update_slice x16, local copies, waits for them, and re-layouts, body(): lax.map(partial(attend_grad, scale=scale), (query_stack, key_stack, value...  61.7 us
    reshape x4, local copies, waits for them, and re-layouts, scatter_pieces(): partial_sum.astype(BF)  57.9 us
    unnamed x163, local copies, waits for them, and re-layouts  56.6 us
  transfers between devices with their start and end apart: 20, of which 16 were waited for; matrix products, arithmetic and copies ran while one was open for 29% of the time, Pallas kernels for 0%

commit v1 on v0

--- a/solution.py
+++ b/solution.py
@@ -242,7 +242,7 @@
     both = jnp.stack([d_gain_one, d_gain_two], 0)
     wide = lax.dynamic_update_slice(jnp.zeros((2, width), F32), both, (0, m_index * width_part))
     small = jnp.concatenate([wide.reshape(-1), d_qgain_part, d_kgain_part])
-    small = lax.psum(small, ALL)
+    small = jnp.sum(lax.all_gather(small, ALL), axis=0)
     wide = small[: 2 * width].reshape(2, width)
     shard = attn_gain.shape[0]
     own = lax.dynamic_slice(wide, (0, (t_index * inner + i_index) * shard), (2, shard))

time: 1430 us -> 1440 us (level)
  blocking collectives: 162 us -> 197 us
  waiting for transfers between devices: 558 us -> 532 us
    all_gather x0 -> x1, blocking collectives: none -> 75.9 us  [body(): small = jnp.sum(lax.all_gather(small, ALL), axis=0)]
    psum x1 -> x0, blocking collectives: 39.7 us -> none  [body(): small = lax.psum(small, ALL)]
    reduce_scatter x4, waiting for transfers between devices: 207 us -> 180 us  [scatter_pieces(): mine = lax.psum_scatter(parts, TP, scatter_dimension=0, tiled=False)]
    unnamed x163 -> x164, local copies, waits for them, and re-layouts: 56.6 us -> 56.6 us
  transfers between devices with their start and end apart: 20 -> 20, of which waited for: 16 -> 15; matrix products, arithmetic and copies ran while one was open for 29% -> 28% of each run, Pallas kernels for 0% -> 0%
where the time goes in v1:
time: 1440 us; the launch traced here: 1430 us
  waiting for transfers between devices  532 us (37%)
  local copies, waits for them, and re-layouts  361 us (25%)
  matrix products  229 us (16%)
  blocking collectives  197 us (14%)
  other arithmetic  77.6 us (5%)
  starting transfers between devices  15.8 us (1%)
  between operations  15.6 us (1%)
    all_gather x4, waiting for transfers between devices, full_rows(): return lax.all_gather(spread(local, inner), 't', axis=0, tiled=True)  221 us
    reduce_scatter x4, waiting for transfers between devices, scatter_pieces(): mine = lax.psum_scatter(parts, TP, scatter_dimension=0, tiled=False)  180 us
    dot_general x17, matrix products, dot_f32(): lax.dot_general(left, right, (dims, ((), ())), preferred_element_type=F32)  176 us
    all_to_all x4, blocking collectives, spread(): parts = lax.all_to_all(parts, 'i', 0, 0, tiled=False)  86.1 us
    all_gather x4, waiting for transfers between devices, gather_pieces(): parts = lax.all_gather(piece, TP, axis=0)  84.7 us
    all_gather x1, blocking collectives, body(): small = jnp.sum(lax.all_gather(small, ALL), axis=0)  75.9 us
    dynamic_update_slice x16, local copies, waits for them, and re-layouts, body(): lax.map(partial(attend_grad, scale=scale), (query_stack, key_stack, value...  61.7 us
    reshape x4, local copies, waits for them, and re-layouts, scatter_pieces(): partial_sum.astype(BF)  57.9 us
  transfers between devices with their start and end apart: 20, of which 15 were waited for; matrix products, arithmetic and copies ran while one was open for 28% of the time, Pallas kernels for 0%

profile of v1, /device:TPU:0, one launch (start us, length us, event | category | flops | bytes accessed | tf_op | source)
XLA Modules:
  0.0 1429.7 jit_solution(14846242864521315863)
XLA Ops:
  27.7 20.5 %all_gather.47 = bf16[2048,2]{0,1:T(2,128)(2,1)S(1)} all-gather(bf16[128,2]{0,1:T(2,128)(2,1)S(1)} %pad_maximum_fusion.6), channel_id=1, replica_groups=mesh['t'=4,'i'=4,'m'=2] {'t','i'}, dimensions={0}, use_global_device_ids=true | all-gather | bytes 8704 | tf_op jit(solution)/shard_map/all_gather | solution.py:153
  50.1 31.7 %all-gather.15.cloned.1.call-done = bf16[2048,640]{0,1:T(8,128)(2,1)} async-done(((bf16[512,640]{0,1:T(8,128)(2,1)}), bf16[2048,640]{0,1:T(8,128)(2,1)}) %all-gather.15.cloned.1.call-update) | async-done | bytes 2621456 | tf_op jit(solution)/shard_map/all_gather | solution.py:114
  81.8 55.0 %all-gather.23.cloned.1.call-done = bf16[4096,1024]{1,0:T(8,128)(2,1)} async-done(((bf16[512,1024]{1,0:T(8,128)(2,1)}), bf16[4096,1024]{1,0:T(8,128)(2,1)}) %all-gather.23.cloned.1.call-update) | async-done | bytes 8388624 | tf_op jit(solution)/shard_map/all_gather | solution.py:87
  153.9 27.7 %copy.137 = f32[4,2,512,1024]{3,1,2,0:T(2,128)S(1)} copy(f32[4,2,512,1024]{3,2,1,0:T(8,128)} %bitcast_convert_fusion) | data formatting | bytes 33554432 | tf_op jit(solution)/shard_map/convert_element_type | solution.py:169
  203.6 16.4 %copy.142 = bf16[4,512,2,1024]{3,2,1,0:T(2,128)(2,1)} copy(bf16[4,512,2,1024]{3,1,2,0:T(8,128)(2,1)} %fusion.58) | data formatting | bytes 16777216 | tf_op jit(solution)/shard_map/mul | solution.py:171
  220.1 14.8 %reshape.765 = bf16[2048,2048,1]{1,0,2:T(8,128)(2,1)} reshape(bf16[4,512,2,1024]{3,2,1,0:T(2,128)(2,1)} %copy.142) | data formatting | bytes 16777216 | tf_op jit(solution)/shard_map/convert_element_type | solution.py:171
  250.3 18.6 %while.26 = (s32[]{:T(128)}, bf16[4,512,4,64]{1,3,2,0:T(8,128)(2,1)}, f32[4,4,512]{2,1,0:T(4,128)}, bf16[4,512,64]{1,2,0:T(8,128)(2,1)S(1)}, pred[4,512,512]{1,2...) while((s32[]{:T(128)}, ...), condition=%wide.region_6.7_spmd, body=%wide.region_3.6_spmd.sunk | while | flops 281147392 | bytes 14617177 | solution.py:185
  278.9 14.5 %reshape.696 = bf16[4,512,2,1024]{3,2,1,0:T(2,128)(2,1)} reshape(bf16[2048,2048]{1,0:T(8,128)(2,1)} %convolution_convert_fusion.2) | data formatting | bytes 16777216 | tf_op jit(solution)/shard_map/reshape | solution.py:94
  303.4 70.8 %reduce-scatter.9.cloned.1.call-done = bf16[1,512,1024]{2,1,0:T(8,128)(2,1)} async-done(((bf16[8,512,1024]{2,1,0:T(8,128)(2,1)}), bf16[1,512,1024]{2,1,0:T(8,128)(2,1)}) %reduce-scatter.9.cloned.1.call-update) | async-done | bytes 1048592 | tf_op jit(solution)/shard_map/reduce_scatter | solution.py:96
  384.2 25.4 %all_to_all.41 = bf16[4,128,1024]{1,2,0:T(8,128)(2,1)S(1)} all-to-all(bf16[4,128,1024]{1,2,0:T(8,128)(2,1)S(1)} %bitcast.453), channel_id=1, replica_groups=mesh['t'=4,'i'=4,'m'=2] {'i'}, dimensions={0} | all-to-all | bytes 2097152 | tf_op jit(solution)/shard_map/all_to_all | solution.py:103
  412.6 28.4 %all_to_all.42 = bf16[4,128,1024]{1,2,0:T(8,128)(2,1)S(1)} all-to-all(bf16[4,128,1024]{1,2,0:T(8,128)(2,1)S(1)} %bitcast.454), channel_id=1, replica_groups=mesh['t'=4,'i'=4,'m'=2] {'i'}, dimensions={0} | all-to-all | bytes 2097152 | tf_op jit(solution)/shard_map/all_to_all | solution.py:103
  442.4 18.0 %all_to_all.43 = bf16[4,128,1024]{1,2,0:T(8,128)(2,1)S(1)} all-to-all(bf16[4,128,1024]{1,2,0:T(8,128)(2,1)} %bitcast.462), channel_id=1, replica_groups=mesh['t'=4,'i'=4,'m'=2] {'i'}, dimensions={0} | all-to-all | bytes 2097152 | tf_op jit(solution)/shard_map/all_to_all | solution.py:103
  461.8 16.7 %copy.155 = bf16[4,2,512,1024]{3,1,2,0:T(2,128)(2,1)} copy(bf16[4,2,512,1024]{3,2,1,0:T(8,128)(2,1)} %bitcast.439) | data formatting | bytes 16777216 | tf_op jit(solution)/shard_map/reshape | solution.py:88
  489.4 18.2 %all-gather.25.cloned.1.call-done = bf16[4096,1024]{1,0:T(8,128)(2,1)} async-done(((bf16[512,1024]{1,0:T(8,128)(2,1)}), bf16[4096,1024]{1,0:T(8,128)(2,1)}) %all-gather.25.cloned.1.call-update) | async-done | bytes 8388624 | tf_op jit(solution)/shard_map/all_gather | solution.py:87
  507.5 16.4 %copy.148 = bf16[4,2,512,1024]{3,1,2,0:T(2,128)(2,1)} copy(bf16[4,2,512,1024]{3,2,1,0:T(8,128)(2,1)} %bitcast.444) | data formatting | bytes 16777216 | tf_op jit(solution)/shard_map/reshape | solution.py:88
  534.2 56.2 %all-gather.17.cloned.1.call-done = bf16[2048,1024]{1,0:T(8,128)(2,1)} async-done(((bf16[512,1024]{1,0:T(8,128)(2,1)}), bf16[2048,1024]{1,0:T(8,128)(2,1)}) %all-gather.17.cloned.1.call-update) | async-done | bytes 4194320 | tf_op jit(solution)/shard_map/all_gather | solution.py:114
  590.4 14.7 %fusion.116 = f32[2048,1024]{1,0:T(8,128)} fusion(bf16[2048,2048]{1,0:T(8,128)(2,1)} %bitcast.440, bf16[2048,1024]{1,0:T(8,128)(2,1)} %all-gather.17.cloned.1.call-done), kind=kOutput, calls=%fused_computation.219 | convolution fusion | flops 8589934592 | bytes 20971520 | tf_op jit(solution)/shard_map/dot_general | solution.py:16
  605.1 66.3 %all-gather.19.cloned.1.call-done = bf16[2048,1024]{1,0:T(8,128)(2,1)} async-done(((bf16[512,1024]{1,0:T(8,128)(2,1)}), bf16[2048,1024]{1,0:T(8,128)(2,1)}) %all-gather.19.cloned.1.call-update) | async-done | bytes 4194320 | tf_op jit(solution)/shard_map/all_gather | solution.py:114
  671.4 14.4 %fusion.117 = f32[2048,1024]{1,0:T(8,128)} fusion(bf16[2048,2048]{1,0:T(8,128)(2,1)} %bitcast.441, bf16[2048,1024]{1,0:T(8,128)(2,1)} %all-gather.19.cloned.1.call-done), kind=kOutput, calls=%fused_computation.220 | convolution fusion | flops 8589934592 | bytes 20971520 | tf_op jit(solution)/shard_map/dot_general | solution.py:16
  685.8 66.6 %all-gather.21.cloned.1.call-done = bf16[2048,1024]{1,0:T(8,128)(2,1)} async-done(((bf16[512,1024]{1,0:T(8,128)(2,1)}), bf16[2048,1024]{1,0:T(8,128)(2,1)}) %all-gather.21.cloned.1.call-update) | async-done | bytes 4194320 | tf_op jit(solution)/shard_map/all_gather | solution.py:114
  752.4 21.8 %multiply_convert_fusion.2 = (bf16[2048,1024]{1,0:T(8,128)(2,1)}, bf16[2048,1024]{1,0:T(8,128)(2,1)}, bf16[2048,1024]{1,0:T(8,128)(2,1)}) fusion(f32[2048,1024]{1,0:T(8,128)} %fusion.116, f32[2048,1024]{1,0:T(8,128)} %fusion.117, bf16[2048,2048]{1,0:T(8,128)(2,1)} %bitcast.437, bf16[2048,1024]{1,0:T(8,128)(2,1)} %all-gather.21.cloned.1.call-done), kind=kOutput, calls=%fused_computation.70 | convolution fusion | flops 8623489024 | bytes 41943040 | tf_op jit(solution)/shard_map/dot_general | solution.py:16
  774.2 14.4 %fusion.118 = f32[2048,2048]{1,0:T(8,128)} fusion(bf16[2048,1024]{1,0:T(8,128)(2,1)} %get-tuple-element.270, bf16[2048,1024]{1,0:T(8,128)(2,1)S(1)} %copy-done.62), kind=kOutput, calls=%fused_computation.221 | convolution fusion | flops 8589934592 | bytes 25165824 | tf_op jit(solution)/shard_map/dot_general | solution.py:16
  788.6 16.4 %add_convert_fusion = bf16[2048,2048]{1,0:T(8,128)(2,1)} fusion(f32[2048,2048]{1,0:T(8,128)} %fusion.118, bf16[2048,1024]{1,0:T(8,128)(2,1)} %get-tuple-element.269, bf16[2048,1024]{1,0:T(8,128)(2,1)} %all-gather.19.cloned.1.call-done), kind=kOutput, calls=%fused_computation.65 | convolution fusion | flops 8598323200 | bytes 33554432 | tf_op jit(solution)/shard_map/dot_general | solution.py:16
  805.0 14.5 %reshape.710 = bf16[4,512,2,1024]{3,2,1,0:T(2,128)(2,1)} reshape(bf16[2048,2048]{1,0:T(8,128)(2,1)} %add_convert_fusion) | data formatting | bytes 16777216 | tf_op jit(solution)/shard_map/reshape | solution.py:94
  828.9 69.9 %reduce-scatter.13.cloned.1.call-done = bf16[1,512,1024]{2,1,0:T(8,128)(2,1)} async-done(((bf16[8,512,1024]{2,1,0:T(8,128)(2,1)}), bf16[1,512,1024]{2,1,0:T(8,128)(2,1)}) %reduce-scatter.13.cloned.1.call-update) | async-done | bytes 1048592 | tf_op jit(solution)/shard_map/reduce_scatter | solution.py:96
  938.8 14.5 %convert_bitcast_fusion = bf16[2048,1024]{0,1:T(8,128)(2,1)} fusion(bf16[2048,1024]{1,0:T(8,128)(2,1)} %get-tuple-element.271, bf16[2048,2048]{1,0:T(8,128)(2,1)} %bitcast.438), kind=kOutput, calls=%fused_computation.77 | convolution fusion | flops 8592031744 | bytes 16777216 | tf_op jit(solution)/shard_map/dot_general | solution.py:16
  964.9 16.4 %copy.157 = bf16[4,2,512,1024]{3,1,2,0:T(2,128)(2,1)} copy(bf16[4,2,512,1024]{3,2,1,0:T(8,128)(2,1)} %bitcast.445) | data formatting | bytes 16777216 | tf_op jit(solution)/shard_map/reshape | solution.py:88
  1004.3 116.4 %while.27 = (s32[]{:T(128)}, f32[4,512,4,64]{1,0,3,2:T(4,128)}, f32[4,512,64]{1,0,2:T(4,128)}, bf16[4,512,64]{1,2,0:T(8,128)(2,1)}, bf16[4,512,64]{1,2,0:T(8,128...) while((s32[]{:T(128)}, f32[4,512,4,64]{1,0,3,2:T(4,128)}, ...), condition=%wide.region_16.17_spmd, body=%wide.region_14.16_spmd.sunk | while | flops 686979072 | bytes 54259364 | solution.py:216
  1154.6 14.5 %reshape.721 = bf16[4,512,2,1024]{3,2,1,0:T(2,128)(2,1)} reshape(bf16[2048,2048]{1,0:T(8,128)(2,1)} %convolution_convert_fusion) | data formatting | bytes 16777216 | tf_op jit(solution)/shard_map/reshape | solution.py:94
  1192.8 14.5 %reshape.706 = bf16[4,512,2,1024]{3,2,1,0:T(2,128)(2,1)} reshape(bf16[2048,2048]{1,0:T(8,128)(2,1)} %convolution_convert_fusion.1) | data formatting | bytes 16777216 | tf_op jit(solution)/shard_map/reshape | solution.py:94
  1293.1 39.7 %reduce-scatter.15.cloned.1.call-done = bf16[1,512,1024]{2,1,0:T(8,128)(2,1)} async-done(((bf16[8,512,1024]{2,1,0:T(8,128)(2,1)}), bf16[1,512,1024]{2,1,0:T(8,128)(2,1)}) %reduce-scatter.15.cloned.1.call-update) | async-done | bytes 1048592 | tf_op jit(solution)/shard_map/reduce_scatter | solution.py:96
  1335.0 75.9 %all-gather.5 = f32[32,1,4224]{2,1,0:T(1,128)} all-gather(f32[1,1,4224]{2,1,0:T(1,128)S(1)} %reshape.756), channel_id=6, replica_groups=mesh['t'=4,'i'=4,'m'=2] {'t','i','m'}, dimensions={0}, use_global_device_ids=true | all-gather | bytes 557568 | tf_op jit(solution)/shard_map/all_gather | solution.py:245
  (399 shorter events, 507.9 us)
Async XLA Ops:
  7.2 74.5 %all-gather.15.cloned.1.call-start = ((), (), s32[]{:S(2)}) async-start(), calls=%async_computation.16 | async-start | bytes 3276800 | tf_op jit(solution)/shard_map/all_gather | solution.py:114
  26.6 110.3 %all-gather.23.cloned.1.call-start = ((), (), s32[]{:S(2)}) async-start(), calls=%async_computation.28 | async-start | bytes 9437184 | tf_op jit(solution)/shard_map/all_gather | solution.py:87
  27.3 346.9 %reduce-scatter.9.cloned.1.call-start = ((), (), s32[]{:S(2)}) async-start(), calls=%async_computation.17 | async-start | bytes 9437184 | tf_op jit(solution)/shard_map/reduce_scatter | solution.py:96
  27.6 213.8 %copy-start.60 = (f32[64]{0:T(128)}, f32[64]{0:T(128)S(1)}, u32[]{:S(2)}) copy-start(f32[64]{0:T(128)S(1)} %convert_element_type.239) | copy-start | bytes 772
  48.2 196.1 %copy-start.58 = (f32[64]{0:T(128)}, f32[64]{0:T(128)S(1)}, u32[]{:S(2)}) copy-start(f32[64]{0:T(128)S(1)} %convert_element_type.247) | copy-start | bytes 772
  49.2 138.4 %copy-start.48 = (f32[2048,1]{0,1:T(1,128)}, f32[2048,1]{0,1:T(1,128)S(1)}, u32[]{:S(2)}) copy-start(f32[2048,1]{0,1:T(1,128)S(1)} %get-tuple-element.297) | copy-start | bytes 24580
  302.7 159.0 %all-gather.27.cloned.1.call-start = ((), (), s32[]{:S(2)}) async-start(), calls=%async_computation.30 | async-start | bytes 9437184 | tf_op jit(solution)/shard_map/all_gather | solution.py:87
  303.3 204.2 %all-gather.25.cloned.1.call-start = ((), (), s32[]{:S(2)}) async-start(), calls=%async_computation.29 | async-start | bytes 9437184 | tf_op jit(solution)/shard_map/all_gather | solution.py:87
  303.4 603.3 %copy-start.44 = (f32[1024,1]{0,1:T(1,128)}, f32[1024,1]{0,1:T(1,128)S(1)}, u32[]{:S(2)}) copy-start(f32[1024,1]{0,1:T(1,128)S(1)} %dynamic-slice_convert_fusion) | copy-start | bytes 12292
  380.8 525.9 %copy-start.50 = (f32[512,1]{0,1:T(1,128)}, f32[512,1]{0,1:T(1,128)S(1)}, u32[]{:S(2)}) copy-start(f32[512,1]{0,1:T(1,128)S(1)} %get-tuple-element.264) | copy-start | bytes 6148
  380.8 525.9 %copy-start.53 = (f32[512,1]{0,1:T(1,128)}, f32[512,1]{0,1:T(1,128)S(1)}, u32[]{:S(2)}) copy-start(f32[512,1]{0,1:T(1,128)S(1)} %get-tuple-element.263) | copy-start | bytes 6148
  383.4 207.0 %all-gather.17.cloned.1.call-start = ((), (), s32[]{:S(2)}) async-start(), calls=%async_computation.18 | async-start | bytes 5242880 | tf_op jit(solution)/shard_map/all_gather | solution.py:114
  410.9 260.5 %all-gather.19.cloned.1.call-start = ((), (), s32[]{:S(2)}) async-start(), calls=%async_computation.19 | async-start | bytes 5242880 | tf_op jit(solution)/shard_map/all_gather | solution.py:114
  442.3 310.0 %all-gather.21.cloned.1.call-start = ((), (), s32[]{:S(2)}) async-start(), calls=%async_computation.20 | async-start | bytes 5242880 | tf_op jit(solution)/shard_map/all_gather | solution.py:114
  461.7 437.2 %reduce-scatter.13.cloned.1.call-start = ((), (), s32[]{:S(2)}) async-start(), calls=%async_computation.22 | async-start | bytes 9437184 | tf_op jit(solution)/shard_map/reduce_scatter | solution.py:96
  828.9 136.0 %all-gather.29.cloned.1.call-start = ((), (), s32[]{:S(2)}) async-start(), calls=%async_computation.31 | async-start | bytes 9437184 | tf_op jit(solution)/shard_map/all_gather | solution.py:87
  910.3 306.3 %reduce-scatter.21.cloned.1.call-start = ((), (), s32[]{:S(2)}) async-start(), calls=%async_computation.26 | async-start | bytes 5242880 | tf_op jit(solution)/shard_map/reduce_scatter | solution.py:118
  924.5 295.9 %reduce-scatter.19.cloned.1.call-start = ((), (), s32[]{:S(2)}) async-start(), calls=%async_computation.25 | async-start | bytes 5242880 | tf_op jit(solution)/shard_map/reduce_scatter | solution.py:118
  938.5 299.8 %reduce-scatter.23.cloned.1.call-start = ((), (), s32[]{:S(2)}) async-start(), calls=%async_computation.27 | async-start | bytes 5242880 | tf_op jit(solution)/shard_map/reduce_scatter | solution.py:118
  953.3 304.8 %reduce-scatter.17.cloned.1.call-start = ((), (), s32[]{:S(2)}) async-start(), calls=%async_computation.24 | async-start | bytes 3276800 | tf_op jit(solution)/shard_map/reduce_scatter | solution.py:118
  1145.6 187.2 %reduce-scatter.15.cloned.1.call-start = ((), (), s32[]{:S(2)}) async-start(), calls=%async_computation.23 | async-start | bytes 9437184 | tf_op jit(solution)/shard_map/reduce_scatter | solution.py:96
  1178.5 239.9 %reduce-scatter.11.cloned.1.call-start = ((), (), s32[]{:S(2)}) async-start(), calls=%async_computation.21 | async-start | bytes 9437184 | tf_op jit(solution)/shard_map/reduce_scatter | solution.py:96
  1216.7 18.1 %all-to-all-start.6 = ((bf16[4,128,1024]{2,1,0:T(8,128)(2,1)}), bf16[4,128,1024]{2,1,0:T(8,128)(2,1)S(1)}, u32[]{:S(2)}, u32[]{:S(2)}) async-start(bf16[4,128,1024]{2,1,0:T(8,128)(2,1)} %bitcast.464), calls=%async_computation.13 | async-start | bytes 2097152 | tf_op jit(solution)/shard_map/all_to_all | solution.py:109
  1234.8 18.0 %all-to-all-start.5 = ((bf16[4,128,1024]{2,1,0:T(8,128)(2,1)}), bf16[4,128,1024]{2,1,0:T(8,128)(2,1)S(1)}, u32[]{:S(2)}, u32[]{:S(2)}) async-start(bf16[4,128,1024]{2,1,0:T(8,128)(2,1)} %bitcast.463), calls=%async_computation.11 | async-start | bytes 2097152 | tf_op jit(solution)/shard_map/all_to_all | solution.py:109
  1252.7 18.0 %all-to-all-start.7 = ((bf16[4,128,1024]{1,2,0:T(8,128)(2,1)}), bf16[4,128,1024]{1,2,0:T(8,128)(2,1)S(1)}, u32[]{:S(2)}, u32[]{:S(2)}) async-start(bf16[4,128,1024]{1,2,0:T(8,128)(2,1)} %copy_bitcast_fusion), calls=%async_computation.15 | async-start | bytes 2097152 | tf_op jit(solution)/shard_map/all_to_all | solution.py:109
  1270.7 14.5 %all-to-all-start.4 = ((bf16[4,128,640]{1,2,0:T(8,128)(2,1)}), bf16[4,128,640]{1,2,0:T(8,128)(2,1)}, u32[]{:S(2)}, u32[]{:S(2)}) async-start(bf16[4,128,640]{1,2,0:T(8,128)(2,1)} %copy_bitcast_fusion.3), calls=%async_computation.9 | async-start | bytes 1310720 | tf_op jit(solution)/shard_map/all_to_all | solution.py:109
  1287.5 130.9 %copy-start.9 = (bf16[1,512,1024]{2,1,0:T(8,128)(2,1)S(1)}, bf16[1,512,1024]{2,1,0:T(8,128)(2,1)}, u32[]{:S(2)}) copy-start(bf16[1,512,1024]{2,1,0:T(8,128)(2,1)} %reduce-scatter.9.cloned.1.call-done) | copy-start | bytes 3145732
  1287.5 130.9 %copy-start.15 = (bf16[512,1024]{1,0:T(8,128)(2,1)S(1)}, bf16[512,1024]{1,0:T(8,128)(2,1)}, u32[]{:S(2)}) copy-start(bf16[512,1024]{1,0:T(8,128)(2,1)} %param.31) | copy-start | bytes 3145732
  1287.5 130.9 %copy-start.45 = (f32[1024,1]{0,1:T(1,128)S(1)}, f32[1024,1]{0,1:T(1,128)}, u32[]{:S(2)}) copy-start(f32[1024,1]{0,1:T(1,128)} %copy-done.44) | copy-start | bytes 12292
  1287.5 130.9 %copy-start.51 = (f32[512,1]{0,1:T(1,128)S(1)}, f32[512,1]{0,1:T(1,128)}, u32[]{:S(2)}) copy-start(f32[512,1]{0,1:T(1,128)} %copy-done.50) | copy-start | bytes 6148
  1287.5 131.0 %copy-start.54 = (f32[512,1]{0,1:T(1,128)S(1)}, f32[512,1]{0,1:T(1,128)}, u32[]{:S(2)}) copy-start(f32[512,1]{0,1:T(1,128)} %copy-done.53) | copy-start | bytes 6148
  1287.5 131.0 %copy-start.56 = (f32[512,1]{0,1:T(1,128)S(1)}, f32[512,1]{0,1:T(1,128)}, u32[]{:S(2)}) copy-start(f32[512,1]{0,1:T(1,128)} %copy-done.55) | copy-start | bytes 6148
  (65 other events, 952.0 us)
Sparse Core Ops, SparseCore 0:
  26.7 55.0 all-gather.14
  83.7 53.1 all-gather.22
  302.9 71.2 reduce-scatter.8
  376.1 74.5 all-gather.26
  453.1 54.3 all-gather.24
  509.6 80.7 all-gather.16
  592.1 79.2 all-gather.18
  673.0 79.2 all-gather.20
  829.0 69.8 reduce-scatter.12
  910.4 54.3 all-gather.28
  967.2 76.7 reduce-scatter.20
  1046.2 77.2 reduce-scatter.18
  1125.8 77.2 reduce-scatter.22
  1205.4 52.5 reduce-scatter.16
  1261.7 70.9 reduce-scatter.14
  1336.1 76.1 reduce-scatter.10
